TPU v7x, 768 devices: a whole 4x8x12 slice. The times are simulated.
768 devices in a mesh: atm: 16 (over y, core), ocn: 48 (over x, z).
Axes of the slice: x: 4, y: 8, z: 12, core: 2. Of those that a mesh axis runs over, the one named last changes fastest.
Arguments:
- phys_flux: bfloat16 [192, 393216], P(None, ('atm', 'ocn')), may hold values from -6 to 6
- send_order: int32 [768, 512], P(('atm', 'ocn')), may hold values from 0 to 511, each once within a row
- near_src: int32 [12288], P(('atm', 'ocn')), may hold values from 0 to 3
- bil_src: int32 [12288, 4], P(('atm', 'ocn')), may hold values from 0 to 3
- nearest_w: bfloat16 [12288, 128, 128], P(('atm', 'ocn')), may hold values from -0.5 to 0.5
- bilinear_w: bfloat16 [12288, 4, 128, 128], P(('atm', 'ocn')), may hold values from -0.25 to 0.25
- owner_step: int32 [12288, 1], P(('atm', 'ocn')), may hold values from 0 to 4; in each aligned block of 16 rows (0 to 15, 16 to 31, ...) at most 4 rows name the same one
- slot: int32 [12288], P(('atm', 'ocn')), may hold values from 0 to 15
Outputs:
- remapped: bfloat16 [192, 1572864], P(None, ('atm', 'ocn'))
- ocean_flux: bfloat16 [12288, 48, 128], P(('atm', 'ocn'))
Inputs may be any that keep to these rules, and one draw needn't show every extreme that they name: `send_order`: each device's row is an ordering of its 512 local columns. `owner_step`: among the 16 target blocks of one device, no value is named more than 4 times, a bound that some block reaches.
All inputs are finite; a program needn't handle non-finite values.
Results may differ from a plain program's by a relative error of at most 0.0044.
Values may be sent and summed in bfloat16 or wider, within the bound.
A program may use at most 32 MiB of HBM per device.

v0:
```python
import jax
import jax.numpy as jnp
from jax import lax
from jax.sharding import PartitionSpec as P

SUB = 4
NWIN = 5
OWN_BLK = 16
CAP = 4


def from_behind(block, axis, distance):
    devices = range(lax.axis_size(axis))
    route = [((i - distance) % len(devices), i) for i in devices]
    return lax.ppermute(block, axis, route)


def local(phys_flux, send_order, near_src, bil_src, nearest_w, bilinear_w, owner_step, slot):
    n_atm = lax.axis_size("atm")
    rows, columns = phys_flux.shape
    width = columns // n_atm
    half = rows // 2
    blk = nearest_w.shape[-1]
    targets = nearest_w.shape[0]
    fields = rows // SUB
    ordered = jnp.take(phys_flux, send_order[0], axis=1).reshape(rows, n_atm, width)
    arrived = lax.all_to_all(ordered, "atm", split_axis=1, concat_axis=1, tiled=True)
    coupler = arrived.reshape(rows, columns)
    blocks = coupler.reshape(rows, columns // blk, blk).transpose(1, 0, 2)
    near = blocks[:, :half][near_src]
    part_n = jnp.einsum("tfc,tcd->tfd", near, nearest_w, preferred_element_type=jnp.float32)
    bil = blocks[:, half:][bil_src]
    part_b = jnp.einsum("tkfc,tkcd->tfd", bil, bilinear_w, preferred_element_type=jnp.float32)
    full = jnp.concatenate([part_n, part_b], axis=1)
    remapped = full.astype(jnp.bfloat16).transpose(1, 0, 2).reshape(rows, targets * blk)
    unit = jnp.mean(full.reshape(targets, fields, SUB, blk), axis=2).astype(jnp.bfloat16)
    capacity = CAP
    reach = NWIN // 2
    step_of = owner_step[:, 0]
    same = step_of[:, None] == step_of[None, :]
    lower = jnp.arange(targets)[None, :] < jnp.arange(targets)[:, None]
    rank = jnp.sum((same & lower).astype(jnp.int32), axis=1)
    position = step_of * capacity + rank
    places = jnp.arange(NWIN * capacity, dtype=jnp.int32)[:, None] == position[None, :]
    packed = jnp.dot(
        places.astype(jnp.bfloat16),
        unit.reshape(targets, fields * blk),
        preferred_element_type=jnp.float32,
    ).astype(jnp.bfloat16)
    packed = packed.reshape(NWIN, capacity, fields * blk)
    filled = jnp.sum(places.astype(jnp.int32), axis=1)
    slot_sent = jnp.where(filled > 0, jnp.sum(places.astype(jnp.int32) * slot[None, :], axis=1), -1)
    slot_sent = slot_sent.reshape(NWIN, capacity)
    unit_parts = [packed[reach]]
    slot_parts = [slot_sent[reach]]
    for offset in range(-reach, reach + 1):
        if offset != 0:
            got_units, got_slots = from_behind(
                (packed[offset + reach], slot_sent[offset + reach]), "ocn", offset
            )
            unit_parts = unit_parts + [got_units]
            slot_parts = slot_parts + [got_slots]
    all_units = jnp.concatenate(unit_parts, axis=0)
    all_slots = jnp.concatenate(slot_parts, axis=0)
    spread = (jnp.arange(OWN_BLK, dtype=jnp.int32)[:, None] == all_slots[None, :]).astype(
        jnp.bfloat16
    )
    summed = jnp.dot(spread, all_units, preferred_element_type=jnp.float32)
    ocean_flux = summed.reshape(OWN_BLK, fields, blk).astype(jnp.bfloat16)
    return (remapped, ocean_flux)


def solution(mesh):
    placed = (
        P(None, ("atm", "ocn")),
        P(("atm", "ocn"), None),
        P(("atm", "ocn")),
        P(("atm", "ocn"), None),
        P(("atm", "ocn"), None, None),
        P(("atm", "ocn"), None, None, None),
        P(("atm", "ocn"), None),
        P(("atm", "ocn")),
    )
    return jax.shard_map(
        local,
        mesh=mesh,
        in_specs=placed,
        out_specs=(P(None, ("atm", "ocn")), P(("atm", "ocn"), None, None)),
        check_vma=False,
    )
```

profile of v0, /device:TPU:16, one launch (start us, length us, event | category | flops | bytes accessed | tf_op | source)
XLA Modules:
  0.0 78.4 jit_solution(7133126356775934572)
XLA Ops:
  0.6 0.0 copy-start
  0.6 0.0 copy-start.5
  0.7 0.0 copy-start.4
  0.7 0.0 copy-start.3
  0.7 1.2 %copy.19 = bf16[192,512]{0,1:T(8,128)(2,1)S(1)} copy(bf16[192,512]{1,0:T(8,128)(2,1)} %param.8) | data formatting | bytes 393216 | tf_op args[0]
  1.9 0.0 copy-start.6
  1.9 0.7 compare_select_fusion.1
  2.6 0.5 broadcast.77
  3.1 1.3 %reduce.3 = s32[512]{0:T(512)S(1)} reduce(s32[1,512]{1,0:T(1,128)} %param.9, s32[]{:T(128)} %broadcast.77), dimensions={0}, to_apply=%param.9.reduce_sub_computation.3 | reduce | bytes 4100 | tf_op args[1]
  4.5 0.1 squeeze.6
  4.5 1.9 %gather_fusion = bf16[512,192]{1,0:T(8,128)(2,1)S(1)} fusion(bf16[192,512]{0,1:T(8,128)(2,1)S(1)} %copy.19, s32[1024]{0:T(1024)S(1)} %pad_clamp_fusion.2), kind=kCustom, calls=%fused_computation | custom fusion | bytes 395264 | tf_op jit(solution)/shard_map/jit(_take)/gather | solution.py:26
  6.5 0.8 %broadcast_select_fusion = bf16[192,16,32]{0,2,1:T(8,128)(2,1)} fusion(bf16[192,16,32]{0,2,1:T(8,128)(2,1)S(1)} %bitcast.36, pred[16,32]{1,0:T(8,128)(4,1)S(1)} %compare_and_fusion), kind=kLoop, calls=%fused_computation.11 | loop fusion | flops 98304 | bytes 393728 | tf_op jit(solution)/shard_map/jit(_take)/select_n | solution.py:26
  7.3 12.7 %all-to-all-start = ((bf16[192,16,32]{0,2,1:T(8,128)(2,1)}), bf16[192,16,32]{0,2,1:T(8,128)(2,1)S(1)}, u32[]{:S(2)}, u32[]{:S(2)}) async-start(bf16[192,16,32]{0,2,1:T(8,128)(2,1)} %broadcast_select_fusion), calls=%async_computation | async-start | bytes 524288 | tf_op jit(solution)/shard_map/all_to_all | solution.py:27
  20.0 0.0 copy-done.5
  20.0 0.2 convert_reduce_fusion.1
  20.2 0.0 copy-done.4
  20.2 0.1 convert_reduce_fusion
  20.3 0.1 fusion.8
  20.4 11.5 %collective-permute-start = (s32[4]{0:T(128)S(1)}, s32[4]{0:T(128)S(1)}, u32[]{:S(2)}, u32[]{:S(2)}) collective-permute-start(s32[4]{0:T(128)S(1)} %get-tuple-element.14), channel_id=1, source_target_pairs={{2,0},{3,1},{4,2},{5,3},{6,4},{7,5},{8,6},{9,7},{10,8},{11,9},{12,... | collective-permute-start | bytes 56 | tf_op jit(solution)/shard_map/ppermute | solution.py:15
  31.9 2.5 %collective-permute-start.1 = (s32[4]{0:T(128)S(1)}, s32[4]{0:T(128)S(1)}, u32[]{:S(2)}, u32[]{:S(2)}) collective-permute-start(s32[4]{0:T(128)S(1)} %get-tuple-element.13), channel_id=1, source_target_pairs={{1,0},{2,1},{3,2},{4,3},{5,4},{6,5},{7,6},{8,7},{9,8},{10,9},{11,1... | collective-permute-start | bytes 56 | tf_op jit(solution)/shard_map/ppermute | solution.py:15
  34.4 3.4 %collective-permute-start.2 = (s32[4]{0:T(128)S(1)}, s32[4]{0:T(128)S(1)}, u32[]{:S(2)}, u32[]{:S(2)}) collective-permute-start(s32[4]{0:T(128)S(1)} %get-tuple-element.12), channel_id=1, source_target_pairs={{47,0},{0,1},{1,2},{2,3},{3,4},{4,5},{5,6},{6,7},{7,8},{8,9},{9,10... | collective-permute-start | bytes 56 | tf_op jit(solution)/shard_map/ppermute | solution.py:15
  37.8 2.8 %collective-permute-start.3 = (s32[4]{0:T(128)S(1)}, s32[4]{0:T(128)S(1)}, u32[]{:S(2)}, u32[]{:S(2)}) collective-permute-start(s32[4]{0:T(128)S(1)} %get-tuple-element.11), channel_id=1, source_target_pairs={{46,0},{47,1},{0,2},{1,3},{2,4},{3,5},{4,6},{5,7},{6,8},{7,9},{8,1... | collective-permute-start | bytes 56 | tf_op jit(solution)/shard_map/ppermute | solution.py:15
  40.6 0.0 copy-done.3
  40.7 0.1 copy.21
  40.7 0.1 reshape.111
  40.8 0.0 copy-done.6
  40.9 0.0 collective-permute-done
  40.9 0.0 collective-permute-done.1
  40.9 2.3 %collective-permute-done.2 = s32[4]{0:T(128)S(1)} collective-permute-done((s32[4]{0:T(128)S(1)}, s32[4]{0:T(128)S(1)}, u32[]{:S(2)}, u32[]{:S(2)}) %collective-permute-start.2) | collective-permute-done | bytes 48 | tf_op jit(solution)/shard_map/ppermute | solution.py:15
  43.2 4.3 %collective-permute-done.3 = s32[4]{0:T(128)S(1)} collective-permute-done((s32[4]{0:T(128)S(1)}, s32[4]{0:T(128)S(1)}, u32[]{:S(2)}, u32[]{:S(2)}) %collective-permute-start.3) | collective-permute-done | bytes 48 | tf_op jit(solution)/shard_map/ppermute | solution.py:15
  47.5 0.1 concatenate.10
  47.6 0.0 all-to-all-done
  47.6 0.2 copy.20
  47.7 1.9 %gather_fusion.2 = bf16[64,96,128]{2,1,0:T(8,128)(2,1)} fusion(bf16[4,96,128]{2,1,0:T(8,128)(2,1)S(1)} %get-tuple-element.10, s32[1024]{0:T(1024)S(1)} %pad_clamp_fusion), kind=kCustom, calls=%fused_computation.2 | custom fusion | bytes 3145984 | tf_op jit(solution)/shard_map/gather | solution.py:32
  49.7 0.0 copy-done
  49.7 2.9 %convolution_bitcast_fusion = f32[16,96,128]{2,1,0:T(8,128)} fusion(bf16[16,4,96,128]{3,2,1,0:T(8,128)(2,1)} %bitcast.33, bf16[16,4,128,128]{3,2,1,0:T(8,128)(2,1)S(1)} %copy-done), kind=kOutput, calls=%fused_computation.6 | convolution fusion | flops 201326592 | bytes 4456448 | tf_op jit(solution)/shard_map/tkfc,tkcd->tfd/dot_general | solution.py:33
  52.5 0.6 gather_fusion.1
  53.2 0.0 copy-start.1
  53.2 1.4 %fusion.9 = f32[16,96,128]{2,1,0:T(8,128)S(1)} fusion(bf16[16,96,128]{2,1,0:T(8,128)(2,1)S(1)} %gather_fusion.1, bf16[16,128,128]{2,1,0:T(8,128)(2,1)} %param.12), kind=kOutput, calls=%fused_computation.36 | convolution fusion | flops 50331648 | bytes 1703936 | tf_op jit(solution)/shard_map/tfc,tcd->tfd/dot_general | solution.py:31
  54.6 0.0 copy-done.1
  54.6 1.3 %pad_maximum_fusion = f32[16,192,128]{2,1,0:T(8,128)} fusion(f32[16,96,128]{2,1,0:T(8,128)S(1)} %copy-done.1, f32[16,96,128]{2,1,0:T(8,128)S(1)} %fusion.9), kind=kLoop, calls=%fused_computation.5 | loop fusion | flops 393216 | bytes 3145728 | tf_op jit(solution)/shard_map/concatenate | solution.py:34
  55.8 2.4 %reduce_sum.39 = f32[16,48,128]{2,1,0:T(8,128)S(1)} reduce(f32[16,48,4,128]{3,2,1,0:T(4,128)} %bitcast.34, f32[]{:T(128)} %constant.14.clone.1), dimensions={2}, to_apply=%region_3.4 | reduce | flops 294912 | bytes 1966084 | tf_op jit(solution)/shard_map/reduce_sum | solution.py:36
  58.2 0.0 copy-start.2
  58.3 0.3 convolution_convert_fusion
  58.6 0.1 fusion.6
  58.7 1.9 %collective-permute-start.4 = (bf16[4,6144]{1,0:T(4,128)(2,1)S(1)}, bf16[4,6144]{1,0:T(4,128)(2,1)S(1)}, u32[]{:S(2)}, u32[]{:S(2)}) collective-permute-start(bf16[4,6144]{1,0:T(4,128)(2,1)S(1)} %get-tuple-element.7), channel_id=1, source_target_pairs={{2,0},{3,1},{4,2},{5,3},{6,4},{7,5},{8,6},{9,7},{10,8},{11,9},{12,... | collective-permute-start | bytes 147464 | tf_op jit(solution)/shard_map/ppermute | solution.py:15
  60.6 2.5 %collective-permute-start.5 = (bf16[4,6144]{1,0:T(4,128)(2,1)S(1)}, bf16[4,6144]{1,0:T(4,128)(2,1)S(1)}, u32[]{:S(2)}, u32[]{:S(2)}) collective-permute-start(bf16[4,6144]{1,0:T(4,128)(2,1)S(1)} %get-tuple-element.6), channel_id=1, source_target_pairs={{1,0},{2,1},{3,2},{4,3},{5,4},{6,5},{7,6},{8,7},{9,8},{10,9},{11,1... | collective-permute-start | bytes 147464 | tf_op jit(solution)/shard_map/ppermute | solution.py:15
  63.1 3.4 %collective-permute-start.6 = (bf16[4,6144]{1,0:T(4,128)(2,1)S(1)}, bf16[4,6144]{1,0:T(4,128)(2,1)S(1)}, u32[]{:S(2)}, u32[]{:S(2)}) collective-permute-start(bf16[4,6144]{1,0:T(4,128)(2,1)S(1)} %get-tuple-element.5), channel_id=1, source_target_pairs={{47,0},{0,1},{1,2},{2,3},{3,4},{4,5},{5,6},{6,7},{7,8},{8,9},{9,10... | collective-permute-start | bytes 147464 | tf_op jit(solution)/shard_map/ppermute | solution.py:15
  66.5 4.8 %collective-permute-start.7 = (bf16[4,6144]{1,0:T(4,128)(2,1)S(1)}, bf16[4,6144]{1,0:T(4,128)(2,1)S(1)}, u32[]{:S(2)}, u32[]{:S(2)}) collective-permute-start(bf16[4,6144]{1,0:T(4,128)(2,1)S(1)} %get-tuple-element.4), channel_id=1, source_target_pairs={{46,0},{47,1},{0,2},{1,3},{2,4},{3,5},{4,6},{5,7},{6,8},{7,9},{8,1... | collective-permute-start | bytes 147464 | tf_op jit(solution)/shard_map/ppermute | solution.py:15
  71.3 0.0 copy-done.2
  71.3 1.0 %copy_bitcast_fusion = bf16[192,2048]{1,0:T(8,128)(2,1)} fusion(f32[16,96,128]{2,1,0:T(8,128)S(1)} %copy-done.2, f32[16,96,128]{2,1,0:T(8,128)S(1)} %fusion.9), kind=kLoop, calls=%fused_computation.8 | loop fusion | flops 1572864 | bytes 2359296 | tf_op jit(solution)/shard_map/reshape | solution.py:35
  72.4 0.0 collective-permute-done.4
  72.4 0.0 collective-permute-done.5
  72.4 0.0 collective-permute-done.6
  72.4 4.9 %collective-permute-done.7 = bf16[4,6144]{1,0:T(4,128)(2,1)S(1)} collective-permute-done((bf16[4,6144]{1,0:T(4,128)(2,1)S(1)}, bf16[4,6144]{1,0:T(4,128)(2,1)S(1)}, u32[]{:S(2)}, u32[]{:S(2)}) %collective-permute-start.7) | collective-permute-done | bytes 49184 | tf_op jit(solution)/shard_map/ppermute | solution.py:15
  77.3 0.2 concatenate.11
  77.5 0.2 fusion
  77.7 0.7 copy.26
  (10 shorter events, 0.1 us)
Async XLA Ops:
  0.6 49.0 %copy-start = (bf16[16,4,128,128]{3,2,1,0:T(8,128)(2,1)S(1)}, bf16[16,4,128,128]{3,2,1,0:T(8,128)(2,1)}, u32[]{:S(2)}) copy-start(bf16[16,4,128,128]{3,2,1,0:T(8,128)(2,1)} %param.13) | copy-start | bytes 6291460
  0.6 19.4 %copy-start.5 = (s32[16,1]{0,1:T(1,128)S(1)}, s32[16,1]{0,1:T(1,128)}, u32[]{:S(2)}) copy-start(s32[16,1]{0,1:T(1,128)} %param.14) | copy-start | bytes 196
  0.7 19.5 %copy-start.4 = (s32[16]{0:T(128)S(1)}, s32[16]{0:T(128)}, u32[]{:S(2)}) copy-start(s32[16]{0:T(128)} %param.15) | copy-start | bytes 196
  0.7 40.0 %copy-start.3 = (s32[16,4]{0,1:T(4,128)S(1)}, s32[16,4]{0,1:T(4,128)}, u32[]{:S(2)}) copy-start(s32[16,4]{0,1:T(4,128)} %param.11) | copy-start | bytes 772
  1.9 39.0 %copy-start.6 = (s32[16]{0:T(128)S(1)}, s32[16]{0:T(128)}, u32[]{:S(2)}) copy-start(s32[16]{0:T(128)} %param.10) | copy-start | bytes 196
  7.3 40.2 %all-to-all-start = ((bf16[192,16,32]{0,2,1:T(8,128)(2,1)}), bf16[192,16,32]{0,2,1:T(8,128)(2,1)S(1)}, u32[]{:S(2)}, u32[]{:S(2)}) async-start(bf16[192,16,32]{0,2,1:T(8,128)(2,1)} %broadcast_select_fusion), calls=%async_computation | async-start | bytes 524288 | tf_op jit(solution)/shard_map/all_to_all | solution.py:27
  20.4 20.5 %collective-permute-start = (s32[4]{0:T(128)S(1)}, s32[4]{0:T(128)S(1)}, u32[]{:S(2)}, u32[]{:S(2)}) collective-permute-start(s32[4]{0:T(128)S(1)} %get-tuple-element.14), channel_id=1, source_target_pairs={{2,0},{3,1},{4,2},{5,3},{6,4},{7,5},{8,6},{9,7},{10,8},{11,9},{12,... | collective-permute-start | bytes 56 | tf_op jit(solution)/shard_map/ppermute | solution.py:15
  31.9 9.0 %collective-permute-start.1 = (s32[4]{0:T(128)S(1)}, s32[4]{0:T(128)S(1)}, u32[]{:S(2)}, u32[]{:S(2)}) collective-permute-start(s32[4]{0:T(128)S(1)} %get-tuple-element.13), channel_id=1, source_target_pairs={{1,0},{2,1},{3,2},{4,3},{5,4},{6,5},{7,6},{8,7},{9,8},{10,9},{11,1... | collective-permute-start | bytes 56 | tf_op jit(solution)/shard_map/ppermute | solution.py:15
  34.4 8.8 %collective-permute-start.2 = (s32[4]{0:T(128)S(1)}, s32[4]{0:T(128)S(1)}, u32[]{:S(2)}, u32[]{:S(2)}) collective-permute-start(s32[4]{0:T(128)S(1)} %get-tuple-element.12), channel_id=1, source_target_pairs={{47,0},{0,1},{1,2},{2,3},{3,4},{4,5},{5,6},{6,7},{7,8},{8,9},{9,10... | collective-permute-start | bytes 56 | tf_op jit(solution)/shard_map/ppermute | solution.py:15
  37.8 9.7 %collective-permute-start.3 = (s32[4]{0:T(128)S(1)}, s32[4]{0:T(128)S(1)}, u32[]{:S(2)}, u32[]{:S(2)}) collective-permute-start(s32[4]{0:T(128)S(1)} %get-tuple-element.11), channel_id=1, source_target_pairs={{46,0},{47,1},{0,2},{1,3},{2,4},{3,5},{4,6},{5,7},{6,8},{7,9},{8,1... | collective-permute-start | bytes 56 | tf_op jit(solution)/shard_map/ppermute | solution.py:15
  53.2 1.4 %copy-start.1 = (f32[16,96,128]{2,1,0:T(8,128)S(1)}, f32[16,96,128]{2,1,0:T(8,128)}, u32[]{:S(2)}) copy-start(f32[16,96,128]{2,1,0:T(8,128)} %convolution_bitcast_fusion) | copy-start | bytes 2359300
  58.2 13.1 %copy-start.2 = (f32[16,96,128]{2,1,0:T(8,128)S(1)}, f32[16,96,128]{2,1,0:T(8,128)}, u32[]{:S(2)}) copy-start(f32[16,96,128]{2,1,0:T(8,128)} %convolution_bitcast_fusion) | copy-start | bytes 2359300
  58.7 13.7 %collective-permute-start.4 = (bf16[4,6144]{1,0:T(4,128)(2,1)S(1)}, bf16[4,6144]{1,0:T(4,128)(2,1)S(1)}, u32[]{:S(2)}, u32[]{:S(2)}) collective-permute-start(bf16[4,6144]{1,0:T(4,128)(2,1)S(1)} %get-tuple-element.7), channel_id=1, source_target_pairs={{2,0},{3,1},{4,2},{5,3},{6,4},{7,5},{8,6},{9,7},{10,8},{11,9},{12,... | collective-permute-start | bytes 147464 | tf_op jit(solution)/shard_map/ppermute | solution.py:15
  60.6 11.7 %collective-permute-start.5 = (bf16[4,6144]{1,0:T(4,128)(2,1)S(1)}, bf16[4,6144]{1,0:T(4,128)(2,1)S(1)}, u32[]{:S(2)}, u32[]{:S(2)}) collective-permute-start(bf16[4,6144]{1,0:T(4,128)(2,1)S(1)} %get-tuple-element.6), channel_id=1, source_target_pairs={{1,0},{2,1},{3,2},{4,3},{5,4},{6,5},{7,6},{8,7},{9,8},{10,9},{11,1... | collective-permute-start | bytes 147464 | tf_op jit(solution)/shard_map/ppermute | solution.py:15
  63.1 9.3 %collective-permute-start.6 = (bf16[4,6144]{1,0:T(4,128)(2,1)S(1)}, bf16[4,6144]{1,0:T(4,128)(2,1)S(1)}, u32[]{:S(2)}, u32[]{:S(2)}) collective-permute-start(bf16[4,6144]{1,0:T(4,128)(2,1)S(1)} %get-tuple-element.5), channel_id=1, source_target_pairs={{47,0},{0,1},{1,2},{2,3},{3,4},{4,5},{5,6},{6,7},{7,8},{8,9},{9,10... | collective-permute-start | bytes 147464 | tf_op jit(solution)/shard_map/ppermute | solution.py:15
  66.5 10.8 %collective-permute-start.7 = (bf16[4,6144]{1,0:T(4,128)(2,1)S(1)}, bf16[4,6144]{1,0:T(4,128)(2,1)S(1)}, u32[]{:S(2)}, u32[]{:S(2)}) collective-permute-start(bf16[4,6144]{1,0:T(4,128)(2,1)S(1)} %get-tuple-element.4), channel_id=1, source_target_pairs={{46,0},{47,1},{0,2},{1,3},{2,4},{3,5},{4,6},{5,7},{6,8},{7,9},{8,1... | collective-permute-start | bytes 147464 | tf_op jit(solution)/shard_map/ppermute | solution.py:15
where the time goes:
time: 79.1 us; the launch traced here: 78.4 us
  starting transfers between devices  45.5 us (58%)
  waiting for transfers between devices  11.5 us (15%)
  other arithmetic  7.88 us (10%)
  local copies, waits for them, and re-layouts  7.75 us (10%)
  matrix products  4.81 us (6%)
  between operations  0.94 us (1%)
    ppermute x8, starting transfers between devices, from_behind(): return lax.ppermute(block, axis, route)  32.8 us
    all_to_all x1, starting transfers between devices, local(): lax.all_to_all(ordered, 'atm', split_axis=1, concat_axis=1, tiled=True)  12.7 us
    ppermute x8, waiting for transfers between devices, from_behind(): return lax.ppermute(block, axis, route)  11.5 us
    dot_general x1, matrix products, local(): jnp.einsum('tkfc,tkcd->tfd', bil, bilinear_w, preferred_element_type=jnp....  2.88 us
    unnamed x17, local copies, waits for them, and re-layouts  2.46 us
    reduce_sum x1, other arithmetic, local(): jnp.mean(full.reshape(targets, fields, SUB, blk), axis=2)  2.35 us
    gather x1, local copies, waits for them, and re-layouts, local(): jnp.take(phys_flux, send_order[0], axis=1).reshape(rows, n_atm, width)  1.95 us
    gather x1, local copies, waits for them, and re-layouts, local(): bil = blocks[:, half:][bil_src]  1.9 us
  transfers between devices with their start and end apart: 9, of which 3 were waited for; matrix products, arithmetic and copies ran while one was open for 2% of the time, Pallas kernels for 0%

commit v1 on v0

v1 whole, which is shorter than its diff:
```python
import functools

import jax
import jax.numpy as jnp
from jax import lax
from jax.experimental import pallas as pl
from jax.experimental.pallas import tpu as pltpu
from jax.sharding import PartitionSpec as P

SUB = 4
NWIN = 5
REACH = NWIN // 2
OWN_BLK = 16
CAP = 4
BLK = 128
ROWS = 192
HALF = 96
COLS = 512
TB = 16
N_ATM = 16
NSB = 4
NBIL = 4
LANES = 128
Q = 32
SEG = 64
GRP = 16
CHUNKS = ((1, 2), (0, 1))
MESH = pl.DeviceIdType.MESH
DISTANCES = (4, 3, 5, 2, 6, 1, 7, 0)
OFFSETS = (0, 4, 1, 3)
UNROLL = 4


def quarter_mask():
    return lax.broadcasted_iota(jnp.int32, (GRP, LANES), 1) // Q


def pick(quarter, values):
    out = values[3]
    for i in (2, 1, 0):
        out = jnp.where(quarter == i, values[i], out)
    return out


def kernel(
    phys, order, near_src, bil_src, near_w, bil_w, step, slot,
    remapped, ocean,
    phys_v, order_v, hot_v, near_wv, bil_wv, near_s, bil_s, step_s, slot_s,
    send_a, send_b, recv_a, recv_b, coupler, full_v, units_v, rem_v,
    pack_a, pack_b, got_a, got_b, slots_v, slots_g, ocean_v,
    in_sem, send_sem, recv_sem, usend_sem, urecv_sem, out_sem,
):
    a, o = lax.axis_index("atm"), lax.axis_index("ocn")
    n_ocn = lax.axis_size("ocn")
    n_chips = N_ATM // 2
    y, core = a // 2, a % 2

    def peer(distance, other):
        return ((y + distance) % n_chips) * 2 + (core + other) % 2

    partners = [(dy, x) for dy in DISTANCES for x in (0, 1) if (dy, x) != (0, 0)]

    def owner(index):
        return (o + (index - REACH) + n_ocn) % n_ocn

    barrier = pltpu.get_barrier_semaphore()
    for dy, x in partners:
        pl.semaphore_signal(barrier, inc=1, device_id=(peer(dy, x), o), device_id_type=MESH)
    for index in OFFSETS:
        pl.semaphore_signal(barrier, inc=1, device_id=(a, owner(index)), device_id_type=MESH)

    loads = [
        pltpu.make_async_copy(src, dst, in_sem.at[i])
        for i, (src, dst) in enumerate(
            [(order, order_v), (phys, phys_v), (step, step_s), (slot, slot_s), (near_src, near_s),
             (bil_src, bil_s), (bil_w, bil_wv), (near_w, near_wv)]
        )
    ]
    for load in loads:
        load.start()

    quarter = quarter_mask()
    loads[0].wait()
    for k in range(0, COLS, LANES):
        for n in range(0, COLS, LANES):
            index = jnp.broadcast_to(order_v[:, n:n + LANES], (LANES, LANES))
            rows = lax.broadcasted_iota(jnp.int32, (LANES, LANES), 0) + k
            hot_v[k:k + LANES, n:n + LANES] = jnp.where(index == rows, 1.0, 0.0).astype(jnp.bfloat16)
    loads[1].wait()
    turn = a % 4
    for chunk, (first, count), send in ((0, CHUNKS[0], send_a), (1, CHUNKS[1], send_b)):
        groups = [
            phys_v[pl.ds(pl.multiple_of((first + u) * SEG + ((q - turn + 4) % 4) * GRP, GRP), GRP), :]
            for u in range(count) for q in range(4)
        ]
        ordered = jnp.dot(jnp.concatenate(groups, axis=0), hot_v[...], preferred_element_type=jnp.float32)
        for u in range(count):
            for g in range(COLS // LANES):
                block = [
                    ordered[(u * 4 + q) * GRP:(u * 4 + q + 1) * GRP, g * LANES:(g + 1) * LANES]
                    for q in range(4)
                ]
                rolled = []
                for shift in range(4):
                    mixed = pick(quarter, [block[(e + shift) % 4] for e in range(4)])
                    rolled.append(pltpu.roll(mixed, shift * Q, 1) if shift else mixed)
                for e in range(4):
                    piece = pick(quarter, [rolled[(q - e) % 4] for q in range(4)])
                    send[g * 4 + e, u] = piece.astype(jnp.bfloat16)

    pl.semaphore_wait(barrier, len(partners) + len(OFFSETS))

    def piece_copy(chunk, dy, x):
        send, recv = ((send_a, recv_a), (send_b, recv_b))[chunk]
        d = peer(dy, x)
        lane = dy * 2 + x
        return pltpu.make_async_remote_copy(
            src_ref=send.at[d], dst_ref=recv.at[a],
            send_sem=send_sem.at[chunk, lane], recv_sem=recv_sem.at[chunk, lane],
            device_id=(d, o), device_id_type=MESH,
        )

    pieces = [[piece_copy(chunk, dy, x) for dy, x in partners] for chunk in range(2)]
    for chunk in range(2):
        for copy in pieces[chunk]:
            copy.start()
    recv_a[a] = send_a[a]
    recv_b[a] = send_b[a]

    for i in (2, 3):
        loads[i].wait()
    steps = [step_s[t] for t in range(TB)]
    places = []
    for t in range(TB):
        rank = jnp.int32(0)
        for before in range(t):
            rank = rank + jnp.where(steps[before] == steps[t], 1, 0)
        places.append(steps[t] * CAP + rank)
    source_of, slot_of = [], []
    for p in range(NWIN * CAP):
        t_of, slot_p = jnp.int32(0), jnp.int32(-1)
        for t in range(TB):
            t_of = jnp.where(places[t] == p, t, t_of)
            slot_p = jnp.where(places[t] == p, slot_s[t], slot_p)
        source_of.append(t_of)
        slot_of.append(slot_p)
    row = lax.broadcasted_iota(jnp.int32, (8, LANES), 0)
    for index in range(NWIN):
        tile = jnp.full((8, LANES), -1, jnp.int32)
        for rank in range(CAP):
            tile = jnp.where(row == rank, slot_of[index * CAP + rank], tile)
        slots_v[index] = tile

    def unit_copy(which, index):
        src, dst = ((pack_a, got_a), (pack_b, got_b), (slots_v, slots_g))[which]
        return pltpu.make_async_remote_copy(
            src_ref=src.at[index], dst_ref=dst.at[index],
            send_sem=usend_sem.at[which, index], recv_sem=urecv_sem.at[which, index],
            device_id=(a, owner(index)), device_id_type=MESH,
        )

    slot_copies = [unit_copy(2, index) for index in OFFSETS]
    for copy in slot_copies:
        copy.start()
    for i in range(4, 8):
        loads[i].wait()

    outs = []
    unit_copies = []
    for chunk, (first, count), recv, pack in (
        (0, CHUNKS[0], recv_a, pack_a), (1, CHUNKS[1], recv_b, pack_b)
    ):
        for copy in pieces[chunk]:
            copy.wait_recv()
        for b in range(NSB):
            for u in range(count):
                parts = [recv[b * 4 + s, u].astype(jnp.float32) for s in range(4)]
                groups = []
                for r in range(4):
                    mixed = pick(quarter, [parts[(q - r) % 4] for q in range(4)])
                    groups.append(pltpu.roll(mixed, (4 - r) * Q, 1) if r else mixed)
                start = (first + u) * SEG
                coupler[b, start:start + SEG, :] = jnp.concatenate(groups, axis=0).astype(jnp.bfloat16)
        low, high = first * SEG, (first + count) * SEG
        near_high, bil_low = min(high, HALF), max(low, HALF)
        fields = (high - low) // SUB

        def targets(i, carry):
            for j in range(UNROLL):
                t = i * UNROLL + j
                lane = pl.ds(pl.multiple_of(t * BLK, BLK), BLK)
                parts = []
                if low < near_high:
                    cells = coupler[near_s[t], low:near_high, :]
                    parts.append(jnp.dot(cells, near_wv[t], preferred_element_type=jnp.float32))
                if bil_low < high:
                    cells = jnp.concatenate(
                        [coupler[bil_s[k, t], bil_low:high, :] for k in range(NBIL)], axis=1
                    )
                    weights = bil_wv[t].reshape(NBIL * BLK, BLK)
                    parts.append(jnp.dot(cells, weights, preferred_element_type=jnp.float32))
                at = 0
                for part in parts:
                    full_v[t, low + at:low + at + part.shape[0], :] = part
                    rem_v[low + at:low + at + part.shape[0], lane] = part.astype(jnp.bfloat16)
                    at += part.shape[0]
                total = full_v[t, pl.ds(low, fields, stride=SUB), :]
                for s in range(1, SUB):
                    total = total + full_v[t, pl.ds(low + s, fields, stride=SUB), :]
                units_v[t, low // SUB:high // SUB, :] = (total * (1.0 / SUB)).astype(jnp.bfloat16)
            return carry

        lax.fori_loop(0, TB // UNROLL, targets, 0)
        for index in (*OFFSETS, REACH):
            for rank in range(CAP):
                pack[index, rank] = units_v[source_of[index * CAP + rank], low // SUB:high // SUB, :]
        copies = [unit_copy(chunk, index) for index in OFFSETS]
        for copy in copies:
            copy.start()
        unit_copies.append(copies)
        out = pltpu.make_async_copy(
            rem_v.at[pl.ds(low, high - low), :], remapped.at[pl.ds(low, high - low), :], out_sem.at[chunk]
        )
        out.start()
        outs.append(out)

    for copy in slot_copies:
        copy.wait_recv()
    for chunk, (first, count), pack, got in (
        (0, CHUNKS[0], pack_a, got_a), (1, CHUNKS[1], pack_b, got_b)
    ):
        low, high = first * SEG // SUB, (first + count) * SEG // SUB
        for copy in unit_copies[chunk]:
            copy.wait_recv()

        def blocks(i, carry):
            for part in range(low, high, GRP):
                sums = [jnp.zeros((GRP, LANES), jnp.float32) for _ in range(UNROLL)]
                for index in range(NWIN):
                    mine = index == REACH
                    for rank in range(CAP):
                        unit = (pack if mine else got)[index, rank, part - low:part - low + GRP, :]
                        unit = unit.astype(jnp.float32)
                        where = (slots_v if mine else slots_g)[index, rank:rank + 1, :]
                        where = jnp.broadcast_to(where, (GRP, LANES))
                        for j in range(UNROLL):
                            sums[j] = sums[j] + jnp.where(where == i * UNROLL + j, unit, 0.0)
                for j in range(UNROLL):
                    ocean_v[i * UNROLL + j, part:part + GRP, :] = sums[j].astype(jnp.bfloat16)
            return carry

        lax.fori_loop(0, OWN_BLK // UNROLL, blocks, 0)
        out = pltpu.make_async_copy(
            ocean_v.at[:, pl.ds(low, high - low), :], ocean.at[:, pl.ds(low, high - low), :],
            out_sem.at[2 + chunk],
        )
        out.start()
        outs.append(out)

    for group in (*pieces, *unit_copies, slot_copies):
        for copy in group:
            copy.wait_send()
    for out in outs:
        out.wait()


def local(phys_flux, send_order, near_src, bil_src, nearest_w, bilinear_w, owner_step, slot):
    any_space = pl.BlockSpec(memory_space=pl.ANY)
    bf16, f32, i32 = jnp.bfloat16, jnp.float32, jnp.int32
    fields = ROWS // SUB
    count_a, count_b = CHUNKS[0][1], CHUNKS[1][1]
    dma = pltpu.SemaphoreType.DMA
    return pl.pallas_call(
        kernel,
        out_shape=(
            jax.ShapeDtypeStruct((ROWS, TB * BLK), bf16),
            jax.ShapeDtypeStruct((OWN_BLK, fields, BLK), bf16),
        ),
        in_specs=[any_space] * 8,
        out_specs=(any_space, any_space),
        scratch_shapes=[
            pltpu.VMEM((ROWS, COLS), bf16),
            pltpu.VMEM((1, COLS), i32),
            pltpu.VMEM((COLS, COLS), bf16),
            pltpu.VMEM((TB, BLK, BLK), bf16),
            pltpu.VMEM((TB, NBIL, BLK, BLK), bf16),
            pltpu.SMEM((TB,), i32),
            pltpu.SMEM((NBIL, TB), i32),
            pltpu.SMEM((TB,), i32),
            pltpu.SMEM((TB,), i32),
            pltpu.VMEM((N_ATM, count_a, GRP, LANES), bf16),
            pltpu.VMEM((N_ATM, count_b, GRP, LANES), bf16),
            pltpu.VMEM((N_ATM, count_a, GRP, LANES), bf16),
            pltpu.VMEM((N_ATM, count_b, GRP, LANES), bf16),
            pltpu.VMEM((NSB, ROWS, BLK), bf16),
            pltpu.VMEM((TB, ROWS, BLK), f32),
            pltpu.VMEM((TB, fields, BLK), bf16),
            pltpu.VMEM((ROWS, TB * BLK), bf16),
            pltpu.VMEM((NWIN, CAP, count_a * GRP, LANES), bf16),
            pltpu.VMEM((NWIN, CAP, count_b * GRP, LANES), bf16),
            pltpu.VMEM((NWIN, CAP, count_a * GRP, LANES), bf16),
            pltpu.VMEM((NWIN, CAP, count_b * GRP, LANES), bf16),
            pltpu.VMEM((NWIN, 8, LANES), i32),
            pltpu.VMEM((NWIN, 8, LANES), i32),
            pltpu.VMEM((OWN_BLK, fields, BLK), bf16),
            dma((8,)),
            dma((2, N_ATM)),
            dma((2, N_ATM)),
            dma((3, NWIN)),
            dma((3, NWIN)),
            dma((4,)),
        ],
        compiler_params=pltpu.CompilerParams(
            collective_id=0, has_side_effects=True, vmem_limit_bytes=67043328
        ),
        name="coupler",
    )(
        phys_flux, send_order, near_src, bil_src.T, nearest_w, bilinear_w, owner_step.reshape(TB), slot
    )


def solution(mesh):
    placed = (
        P(None, ("atm", "ocn")),
        P(("atm", "ocn"), None),
        P(("atm", "ocn")),
        P(("atm", "ocn"), None),
        P(("atm", "ocn"), None, None),
        P(("atm", "ocn"), None, None, None),
        P(("atm", "ocn"), None),
        P(("atm", "ocn")),
    )
    return jax.shard_map(
        local,
        mesh=mesh,
        in_specs=placed,
        out_specs=(P(None, ("atm", "ocn")), P(("atm", "ocn"), None, None)),
        check_vma=False,
    )
```

time: 79.1 us -> 39.4 us (0.50)
  the two profiles are of different devices: /device:TPU:16 before, /device:TPU:1 now
where the time goes in v1:
time: 39.4 us; the launch traced here: 39.2 us
  Pallas kernels  34.8 us (88%)
  local copies, waits for them, and re-layouts  3.7 us (9%)
  between operations  0.64 us (2%)
    pallas_call x1, Pallas kernels, local(): pl.pallas_call(kernel, out_shape=(jax.ShapeDtypeStruct((ROWS, TB * BLK),...  34.8 us
    unnamed x2, local copies, waits for them, and re-layouts  3.7 us

profile of v1, /device:TPU:1, one launch (start us, length us, event | category | flops | bytes accessed | tf_op | source)
XLA Modules:
  0.0 39.2 jit_solution(10717433287567338282)
XLA Ops:
  0.6 34.8 %coupler.1 = (bf16[192,2048]{1,0:T(8,128)(2,1)}, bf16[16,48,128]{2,1,0:T(8,128)(2,1)}) custom-call(bf16[192,512]{1,0:T(8,128)(2,1)} %phys.1, s32[1,512]{1,0:T(1,128)} %order.1, s32[16]{0:T(128)} %near_src.1, s32[4,16]{1,0:T(4,128)} %bitcast.2, bf16[16,128,128]{2,1,0:T(8,128)(2,1)} %near_w.1, bf16[16,4,128,128]{3,2,1,0:T(8,128)(2,1)} %bil_w.1, s32[16]{0:T(128)} %bitcast.3, ...), custom_call_target="tpu_custom_call" | custom-call | tf_op jit(solution)/shard_map/coupler/pallas_call | solution.py:273
  35.5 2.1 %copy.12 = bf16[192,2048]{1,0:T(8,128)(2,1)} copy(bf16[192,2048]{1,0:T(8,128)(2,1)} %get-tuple-element.4) | data formatting | bytes 1572864
  37.6 1.6 %copy.13 = bf16[16,48,128]{2,1,0:T(8,128)(2,1)} copy(bf16[16,48,128]{2,1,0:T(8,128)(2,1)} %get-tuple-element.5) | data formatting | bytes 393216

commit v2 on v1

v2 whole, which is shorter than its diff:
```python
import functools

import jax
import jax.numpy as jnp
from jax import lax
from jax.experimental import pallas as pl
from jax.experimental.pallas import tpu as pltpu
from jax.sharding import PartitionSpec as P

SUB = 4
NWIN = 5
REACH = NWIN // 2
OWN_BLK = 16
CAP = 4
BLK = 128
ROWS = 192
HALF = 96
COLS = 512
TB = 16
N_ATM = 16
NSB = 4
NBIL = 4
LANES = 128
Q = 32
SEG = 64
GRP = 16
CHUNKS = (2, 1, 0)
MESH = pl.DeviceIdType.MESH
DISTANCES = (4, 3, 5, 2, 6, 1, 7, 0)
OFFSETS = (0, 4, 1, 3)
UNROLL = 4


def quarter_mask():
    return lax.broadcasted_iota(jnp.int32, (GRP, LANES), 1) // Q


def pick(quarter, values):
    out = values[3]
    for i in (2, 1, 0):
        out = jnp.where(quarter == i, values[i], out)
    return out


def kernel(
    phys, order, near_src, bil_src, near_w, bil_w, step, slot,
    remapped, ocean,
    phys_v, order_v, hot_v, near_wv, bil_wv, near_s, bil_s, step_s, slot_s,
    send, recv, coupler, full_v, units_v, pack, got, slots_v, slots_g,
    in_sem, send_sem, recv_sem, usend_sem, urecv_sem,
):
    a, o = lax.axis_index("atm"), lax.axis_index("ocn")
    n_ocn = lax.axis_size("ocn")
    n_chips = N_ATM // 2
    y, core = a // 2, a % 2

    def peer(distance, other):
        return ((y + distance) % n_chips) * 2 + (core + other) % 2

    partners = [(dy, x) for dy in DISTANCES for x in (0, 1) if (dy, x) != (0, 0)]

    def owner(index):
        return (o + (index - REACH) + n_ocn) % n_ocn

    barrier = pltpu.get_barrier_semaphore()
    for dy, x in partners:
        pl.semaphore_signal(barrier, inc=1, device_id=(peer(dy, x), o), device_id_type=MESH)
    for index in OFFSETS:
        pl.semaphore_signal(barrier, inc=1, device_id=(a, owner(index)), device_id_type=MESH)

    loads = [
        pltpu.make_async_copy(src, dst, in_sem.at[i])
        for i, (src, dst) in enumerate(
            [(order, order_v), (phys, phys_v), (step, step_s), (slot, slot_s), (near_src, near_s),
             (bil_src, bil_s), (bil_w, bil_wv), (near_w, near_wv)]
        )
    ]
    for load in loads:
        load.start()

    quarter = quarter_mask()
    loads[0].wait()
    for k in range(0, COLS, LANES):
        for n in range(0, COLS, LANES):
            index = jnp.broadcast_to(order_v[:, n:n + LANES], (LANES, LANES))
            rows = lax.broadcasted_iota(jnp.int32, (LANES, LANES), 0) + k
            hot_v[k:k + LANES, n:n + LANES] = jnp.where(index == rows, 1.0, 0.0).astype(jnp.bfloat16)
    loads[1].wait()
    turn = a % 4
    groups = [
        phys_v[pl.ds(pl.multiple_of(segment * SEG + ((q - turn + 4) % 4) * GRP, GRP), GRP), :]
        for segment in CHUNKS for q in range(4)
    ]
    ordered = jnp.dot(jnp.concatenate(groups, axis=0), hot_v[...], preferred_element_type=jnp.float32)
    for chunk in range(len(CHUNKS)):
        for g in range(COLS // LANES):
            block = [
                ordered[(chunk * 4 + q) * GRP:(chunk * 4 + q + 1) * GRP, g * LANES:(g + 1) * LANES]
                for q in range(4)
            ]
            rolled = []
            for shift in range(4):
                mixed = pick(quarter, [block[(e + shift) % 4] for e in range(4)])
                rolled.append(pltpu.roll(mixed, shift * Q, 1) if shift else mixed)
            for e in range(4):
                piece = pick(quarter, [rolled[(q - e) % 4] for q in range(4)])
                send[chunk, g * 4 + e] = piece.astype(jnp.bfloat16)

    pl.semaphore_wait(barrier, len(partners) + len(OFFSETS))

    def piece_copy(chunk, dy, x):
        d = peer(dy, x)
        lane = dy * 2 + x
        return pltpu.make_async_remote_copy(
            src_ref=send.at[chunk, d], dst_ref=recv.at[chunk, a],
            send_sem=send_sem.at[chunk, lane], recv_sem=recv_sem.at[chunk, lane],
            device_id=(d, o), device_id_type=MESH,
        )

    pieces = [[piece_copy(chunk, dy, x) for dy, x in partners] for chunk in range(len(CHUNKS))]
    for group in pieces:
        for copy in group:
            copy.start()
    for chunk in range(len(CHUNKS)):
        recv[chunk, a] = send[chunk, a]

    for i in (2, 3):
        loads[i].wait()
    steps = [step_s[t] for t in range(TB)]
    places = []
    for t in range(TB):
        rank = jnp.int32(0)
        for before in range(t):
            rank = rank + jnp.where(steps[before] == steps[t], 1, 0)
        places.append(steps[t] * CAP + rank)
    source_of, slot_of = [], []
    for p in range(NWIN * CAP):
        t_of, slot_p = jnp.int32(0), jnp.int32(-1)
        for t in range(TB):
            t_of = jnp.where(places[t] == p, t, t_of)
            slot_p = jnp.where(places[t] == p, slot_s[t], slot_p)
        source_of.append(t_of)
        slot_of.append(slot_p)
    row = lax.broadcasted_iota(jnp.int32, (8, LANES), 0)
    for index in range(NWIN):
        tile = jnp.full((8, LANES), -1, jnp.int32)
        for rank in range(CAP):
            tile = jnp.where(row == rank, slot_of[index * CAP + rank], tile)
        slots_v[index] = tile

    def owner_copy(src, dst, which, index):
        return pltpu.make_async_remote_copy(
            src_ref=src, dst_ref=dst,
            send_sem=usend_sem.at[which, index], recv_sem=urecv_sem.at[which, index],
            device_id=(a, owner(index)), device_id_type=MESH,
        )

    slot_copies = [owner_copy(slots_v.at[i], slots_g.at[i], len(CHUNKS), i) for i in OFFSETS]
    for copy in slot_copies:
        copy.start()
    for i in range(4, 8):
        loads[i].wait()

    unit_copies = []
    for chunk, segment in enumerate(CHUNKS):
        for copy in pieces[chunk]:
            copy.wait_recv()
        low, high = segment * SEG, (segment + 1) * SEG
        for b in range(NSB):
            parts = [recv[chunk, b * 4 + s].astype(jnp.float32) for s in range(4)]
            groups = []
            for r in range(4):
                mixed = pick(quarter, [parts[(q - r) % 4] for q in range(4)])
                groups.append(pltpu.roll(mixed, (4 - r) * Q, 1) if r else mixed)
            coupler[b, low:high, :] = jnp.concatenate(groups, axis=0).astype(jnp.bfloat16)
        near_high, bil_low = min(high, HALF), max(low, HALF)
        fields = SEG // SUB

        def targets(i, carry):
            for j in range(UNROLL):
                t = i * UNROLL + j
                lane = pl.ds(pl.multiple_of(t * BLK, BLK), BLK)
                parts = []
                if low < near_high:
                    cells = coupler[near_s[t], low:near_high, :]
                    parts.append(jnp.dot(cells, near_wv[t], preferred_element_type=jnp.float32))
                if bil_low < high:
                    cells = jnp.concatenate(
                        [coupler[bil_s[k, t], bil_low:high, :] for k in range(NBIL)], axis=1
                    )
                    weights = bil_wv[t].reshape(NBIL * BLK, BLK)
                    parts.append(jnp.dot(cells, weights, preferred_element_type=jnp.float32))
                at = 0
                for part in parts:
                    full_v[t, low + at:low + at + part.shape[0], :] = part
                    remapped[low + at:low + at + part.shape[0], lane] = part.astype(jnp.bfloat16)
                    at += part.shape[0]
                total = full_v[t, pl.ds(low, fields, stride=SUB), :]
                for s in range(1, SUB):
                    total = total + full_v[t, pl.ds(low + s, fields, stride=SUB), :]
                units_v[t, low // SUB:high // SUB, :] = (total * (1.0 / SUB)).astype(jnp.bfloat16)
            return carry

        lax.fori_loop(0, TB // UNROLL, targets, 0)
        for index in (*OFFSETS, REACH):
            for rank in range(CAP):
                pack[chunk, index, rank] = units_v[source_of[index * CAP + rank], low // SUB:high // SUB, :]
        copies = [owner_copy(pack.at[chunk, i], got.at[chunk, i], chunk, i) for i in OFFSETS]
        for copy in copies:
            copy.start()
        unit_copies.append(copies)

    for copy in slot_copies:
        copy.wait_recv()
    for chunk, segment in enumerate(CHUNKS):
        low = segment * GRP
        for copy in unit_copies[chunk]:
            copy.wait_recv()

        def blocks(i, carry):
            sums = [jnp.zeros((GRP, LANES), jnp.float32) for _ in range(UNROLL)]
            for index in range(NWIN):
                mine = index == REACH
                for rank in range(CAP):
                    unit = (pack if mine else got)[chunk, index, rank].astype(jnp.float32)
                    where = (slots_v if mine else slots_g)[index, rank:rank + 1, :]
                    where = jnp.broadcast_to(where, (GRP, LANES))
                    for j in range(UNROLL):
                        sums[j] = sums[j] + jnp.where(where == i * UNROLL + j, unit, 0.0)
            for j in range(UNROLL):
                ocean[i * UNROLL + j, low:low + GRP, :] = sums[j].astype(jnp.bfloat16)
            return carry

        lax.fori_loop(0, OWN_BLK // UNROLL, blocks, 0)

    for group in (*pieces, *unit_copies, slot_copies):
        for copy in group:
            copy.wait_send()


def write(remapped, ocean, remapped_out, ocean_out, sem):
    copies = [
        pltpu.make_async_copy(remapped, remapped_out, sem.at[0]),
        pltpu.make_async_copy(ocean, ocean_out, sem.at[1]),
    ]
    for copy in copies:
        copy.start()
    for copy in copies:
        copy.wait()


def local(phys_flux, send_order, near_src, bil_src, nearest_w, bilinear_w, owner_step, slot):
    bf16, f32, i32 = jnp.bfloat16, jnp.float32, jnp.int32
    fields, chunks = ROWS // SUB, len(CHUNKS)
    dma = pltpu.SemaphoreType.DMA
    hbm = pl.BlockSpec(memory_space=pltpu.HBM)
    vmem = pl.BlockSpec(memory_space=pltpu.VMEM)
    args = (
        phys_flux, send_order, near_src, bil_src.T, nearest_w, bilinear_w, owner_step.reshape(TB), slot
    )
    results = pl.pallas_call(
        kernel,
        out_shape=(
            pltpu.VMEM((ROWS, TB * BLK), bf16),
            pltpu.VMEM((OWN_BLK, fields, BLK), bf16),
        ),
        in_specs=[hbm] * 8,
        out_specs=(vmem, vmem),
        scratch_shapes=[
            pltpu.VMEM((ROWS, COLS), bf16),
            pltpu.VMEM((1, COLS), i32),
            pltpu.VMEM((COLS, COLS), bf16),
            pltpu.VMEM((TB, BLK, BLK), bf16),
            pltpu.VMEM((TB, NBIL, BLK, BLK), bf16),
            pltpu.SMEM((TB,), i32),
            pltpu.SMEM((NBIL, TB), i32),
            pltpu.SMEM((TB,), i32),
            pltpu.SMEM((TB,), i32),
            pltpu.VMEM((chunks, N_ATM, GRP, LANES), bf16),
            pltpu.VMEM((chunks, N_ATM, GRP, LANES), bf16),
            pltpu.VMEM((NSB, ROWS, BLK), bf16),
            pltpu.VMEM((TB, ROWS, BLK), f32),
            pltpu.VMEM((TB, fields, BLK), bf16),
            pltpu.VMEM((chunks, NWIN, CAP, GRP, LANES), bf16),
            pltpu.VMEM((chunks, NWIN, CAP, GRP, LANES), bf16),
            pltpu.VMEM((NWIN, 8, LANES), i32),
            pltpu.VMEM((NWIN, 8, LANES), i32),
            dma((8,)),
            dma((chunks, N_ATM)),
            dma((chunks, N_ATM)),
            dma((chunks + 1, NWIN)),
            dma((chunks + 1, NWIN)),
        ],
        compiler_params=pltpu.CompilerParams(
            collective_id=0, has_side_effects=True, vmem_limit_bytes=24 << 20
        ),
        name="coupler",
    )(*[pltpu.with_memory_space_constraint(x, pltpu.HBM) for x in args])
    return pl.pallas_call(
        write,
        out_shape=(
            pltpu.HBM((ROWS, TB * BLK), bf16),
            pltpu.HBM((OWN_BLK, fields, BLK), bf16),
        ),
        in_specs=[vmem, vmem],
        out_specs=(hbm, hbm),
        scratch_shapes=[dma((2,))],
        compiler_params=pltpu.CompilerParams(vmem_limit_bytes=1 << 20),
        name="write",
    )(*[pltpu.with_memory_space_constraint(x, pltpu.VMEM) for x in results])


def solution(mesh):
    placed = (
        P(None, ("atm", "ocn")),
        P(("atm", "ocn"), None),
        P(("atm", "ocn")),
        P(("atm", "ocn"), None),
        P(("atm", "ocn"), None, None),
        P(("atm", "ocn"), None, None, None),
        P(("atm", "ocn"), None),
        P(("atm", "ocn")),
    )
    return jax.shard_map(
        local,
        mesh=mesh,
        in_specs=placed,
        out_specs=(P(None, ("atm", "ocn")), P(("atm", "ocn"), None, None)),
        check_vma=False,
    )
```

time: 39.4 us -> 34.8 us (0.88)
  local copies, waits for them, and re-layouts: 3.7 us -> 0 us
  Pallas kernels: 34.8 us -> 34 us
    unnamed x2 -> x0, local copies, waits for them, and re-layouts: 3.7 us -> none
    pallas_call x1 -> x2, Pallas kernels: 34.8 us -> 34 us  [the longest x1 33.1 us: local(): pl.pallas_call(kernel, out_shape=(pltpu.VMEM((ROWS, TB * BLK), bf16), plt...]
where the time goes in v2:
time: 34.8 us; the launch traced here: 34.7 us
  Pallas kernels  34 us (98%)
  between operations  0.64 us (2%)
    pallas_call x1, Pallas kernels, local(): pl.pallas_call(kernel, out_shape=(pltpu.VMEM((ROWS, TB * BLK), bf16), plt...  33.1 us
    pallas_call x1, Pallas kernels, local(): pl.pallas_call(write, out_shape=(pltpu.HBM((ROWS, TB * BLK), bf16), pltpu...  0.96 us

profile of v2, /device:TPU:1, one launch (start us, length us, event | category | flops | bytes accessed | tf_op | source)
XLA Modules:
  0.0 34.7 jit_solution(9483547128216736933)
XLA Ops:
  0.6 33.1 %coupler.1 = (bf16[192,2048]{1,0:T(8,128)(2,1)S(1)}, bf16[16,48,128]{2,1,0:T(8,128)(2,1)S(1)}) custom-call(bf16[192,512]{1,0:T(8,128)(2,1)} %phys.1, s32[1,512]{1,0:T(1,128)} %order.1, s32[16]{0:T(128)} %near_src.1, s32[4,16]{1,0:T(4,128)} %bitcast.2, bf16[16,128,128]{2,1,0:T(8,128)(2,1)} %near_w.1, bf16[16,4,128,128]{3,2,1,0:T(8,128)(2,1)} %bil_w.1, ...), custom_call_target="tpu_custom_call" | custom-call | tf_op jit(solution)/shard_map/coupler/pallas_call | solution.py:261
  33.7 1.0 %write.1 = (bf16[192,2048]{1,0:T(8,128)(2,1)}, bf16[16,48,128]{2,1,0:T(8,128)(2,1)}) custom-call(bf16[192,2048]{1,0:T(8,128)(2,1)S(1)} %get-tuple-element.4.remapped, bf16[16,48,128]{2,1,0:T(8,128)(2,1)S(1)} %get-tuple-element.5.ocean), custom_call_target="tpu_custom_call" | custom-call | tf_op jit(solution)/shard_map/write/pallas_call | solution.py:299

commit v3 on v2

--- a/solution.py
+++ b/solution.py
@@ -46,7 +46,7 @@
     phys, order, near_src, bil_src, near_w, bil_w, step, slot,
     remapped, ocean,
     phys_v, order_v, hot_v, near_wv, bil_wv, near_s, bil_s, step_s, slot_s,
-    send, recv, coupler, full_v, units_v, pack, got, slots_v, slots_g,
+    send, recv, coupler, full_v, units_v, pack, got, slots_v, slots_g, total_v,
     in_sem, send_sem, recv_sem, usend_sem, urecv_sem,
 ):
     a, o = lax.axis_index("atm"), lax.axis_index("ocn")
@@ -176,10 +176,9 @@
         near_high, bil_low = min(high, HALF), max(low, HALF)
         fields = SEG // SUB
 
-        def targets(i, carry):
-            for j in range(UNROLL):
-                t = i * UNROLL + j
-                lane = pl.ds(pl.multiple_of(t * BLK, BLK), BLK)
+        def targets():
+            for t in range(TB):
+                lane = slice(t * BLK, (t + 1) * BLK)
                 parts = []
                 if low < near_high:
                     cells = coupler[near_s[t], low:near_high, :]
@@ -199,9 +198,8 @@
                 for s in range(1, SUB):
                     total = total + full_v[t, pl.ds(low + s, fields, stride=SUB), :]
                 units_v[t, low // SUB:high // SUB, :] = (total * (1.0 / SUB)).astype(jnp.bfloat16)
-            return carry
-
-        lax.fori_loop(0, TB // UNROLL, targets, 0)
+
+        targets()
         for index in (*OFFSETS, REACH):
             for rank in range(CAP):
                 pack[chunk, index, rank] = units_v[source_of[index * CAP + rank], low // SUB:high // SUB, :]
@@ -214,24 +212,26 @@
         copy.wait_recv()
     for chunk, segment in enumerate(CHUNKS):
         low = segment * GRP
-        for copy in unit_copies[chunk]:
-            copy.wait_recv()
-
-        def blocks(i, carry):
-            sums = [jnp.zeros((GRP, LANES), jnp.float32) for _ in range(UNROLL)]
-            for index in range(NWIN):
-                mine = index == REACH
-                for rank in range(CAP):
-                    unit = (pack if mine else got)[chunk, index, rank].astype(jnp.float32)
-                    where = (slots_v if mine else slots_g)[index, rank:rank + 1, :]
-                    where = jnp.broadcast_to(where, (GRP, LANES))
-                    for j in range(UNROLL):
-                        sums[j] = sums[j] + jnp.where(where == i * UNROLL + j, unit, 0.0)
-            for j in range(UNROLL):
-                ocean[i * UNROLL + j, low:low + GRP, :] = sums[j].astype(jnp.bfloat16)
-            return carry
-
-        lax.fori_loop(0, OWN_BLK // UNROLL, blocks, 0)
+        for stage, indices in enumerate(((2, 1, 3), (0, 4))):
+            for copy, index in zip(unit_copies[chunk], OFFSETS):
+                if index in indices:
+                    copy.wait_recv()
+            for first in range(0, OWN_BLK, UNROLL):
+                wanted = range(first, first + UNROLL)
+                sums = [total_v[i] if stage else jnp.zeros((GRP, LANES), jnp.float32) for i in wanted]
+                for index in indices:
+                    mine = index == REACH
+                    for rank in range(CAP):
+                        unit = (pack if mine else got)[chunk, index, rank].astype(jnp.float32)
+                        where = (slots_v if mine else slots_g)[index, rank:rank + 1, :]
+                        where = jnp.broadcast_to(where, (GRP, LANES))
+                        for j, i in enumerate(wanted):
+                            sums[j] = sums[j] + jnp.where(where == i, unit, 0.0)
+                for j, i in enumerate(wanted):
+                    if stage:
+                        ocean[i, low:low + GRP, :] = sums[j].astype(jnp.bfloat16)
+                    else:
+                        total_v[i] = sums[j]
 
     for group in (*pieces, *unit_copies, slot_copies):
         for copy in group:
@@ -285,6 +285,7 @@
             pltpu.VMEM((chunks, NWIN, CAP, GRP, LANES), bf16),
             pltpu.VMEM((NWIN, 8, LANES), i32),
             pltpu.VMEM((NWIN, 8, LANES), i32),
+            pltpu.VMEM((OWN_BLK, GRP, LANES), f32),
             dma((8,)),
             dma((chunks, N_ATM)),
             dma((chunks, N_ATM)),

time: 34.8 us -> 34.2 us (0.983)
  Pallas kernels: 34 us -> 33.4 us
    pallas_call x1, Pallas kernels: 33.1 us -> 32.5 us  [local(): pl.pallas_call(kernel, out_shape=(pltpu.VMEM((ROWS, TB * BLK), bf16), plt...]
where the time goes in v3:
time: 34.2 us; the launch traced here: 34.1 us
  Pallas kernels  33.4 us (98%)
  between operations  0.64 us (2%)
    pallas_call x1, Pallas kernels, local(): pl.pallas_call(kernel, out_shape=(pltpu.VMEM((ROWS, TB * BLK), bf16), plt...  32.5 us
    pallas_call x1, Pallas kernels, local(): pl.pallas_call(write, out_shape=(pltpu.HBM((ROWS, TB * BLK), bf16), pltpu...  0.96 us

profile of v3, /device:TPU:1, one launch (start us, length us, event | category | flops | bytes accessed | tf_op | source)
XLA Modules:
  0.0 34.1 jit_solution(16488839106845510435)
XLA Ops:
  0.6 32.5 %coupler.1 = (bf16[192,2048]{1,0:T(8,128)(2,1)S(1)}, bf16[16,48,128]{2,1,0:T(8,128)(2,1)S(1)}) custom-call(bf16[192,512]{1,0:T(8,128)(2,1)} %phys.1, s32[1,512]{1,0:T(1,128)} %order.1, s32[16]{0:T(128)} %near_src.1, s32[4,16]{1,0:T(4,128)} %bitcast.2, bf16[16,128,128]{2,1,0:T(8,128)(2,1)} %near_w.1, bf16[16,4,128,128]{3,2,1,0:T(8,128)(2,1)} %bil_w.1, ...), custom_call_target="tpu_custom_call" | custom-call | tf_op jit(solution)/shard_map/coupler/pallas_call | solution.py:261
  33.1 1.0 %write.1 = (bf16[192,2048]{1,0:T(8,128)(2,1)}, bf16[16,48,128]{2,1,0:T(8,128)(2,1)}) custom-call(bf16[192,2048]{1,0:T(8,128)(2,1)S(1)} %get-tuple-element.4.remapped, bf16[16,48,128]{2,1,0:T(8,128)(2,1)S(1)} %get-tuple-element.5.ocean), custom_call_target="tpu_custom_call" | custom-call | tf_op jit(solution)/shard_map/write/pallas_call | solution.py:300

commit v4 on v3

--- a/solution.py
+++ b/solution.py
@@ -87,17 +87,15 @@
             hot_v[k:k + LANES, n:n + LANES] = jnp.where(index == rows, 1.0, 0.0).astype(jnp.bfloat16)
     loads[1].wait()
     turn = a % 4
-    groups = [
-        phys_v[pl.ds(pl.multiple_of(segment * SEG + ((q - turn + 4) % 4) * GRP, GRP), GRP), :]
-        for segment in CHUNKS for q in range(4)
-    ]
-    ordered = jnp.dot(jnp.concatenate(groups, axis=0), hot_v[...], preferred_element_type=jnp.float32)
-    for chunk in range(len(CHUNKS)):
+
+    def arrange(chunk):
+        start = CHUNKS[chunk] * SEG
+        groups = [
+            phys_v[pl.ds(pl.multiple_of(start + ((q - turn + 4) % 4) * GRP, GRP), GRP), :] for q in range(4)
+        ]
+        ordered = jnp.dot(jnp.concatenate(groups, axis=0), hot_v[...], preferred_element_type=jnp.float32)
         for g in range(COLS // LANES):
-            block = [
-                ordered[(chunk * 4 + q) * GRP:(chunk * 4 + q + 1) * GRP, g * LANES:(g + 1) * LANES]
-                for q in range(4)
-            ]
+            block = [ordered[q * GRP:(q + 1) * GRP, g * LANES:(g + 1) * LANES] for q in range(4)]
             rolled = []
             for shift in range(4):
                 mixed = pick(quarter, [block[(e + shift) % 4] for e in range(4)])
@@ -106,6 +104,7 @@
                 piece = pick(quarter, [rolled[(q - e) % 4] for q in range(4)])
                 send[chunk, g * 4 + e] = piece.astype(jnp.bfloat16)
 
+    arrange(0)
     pl.semaphore_wait(barrier, len(partners) + len(OFFSETS))
 
     def piece_copy(chunk, dy, x):
@@ -118,7 +117,9 @@
         )
 
     pieces = [[piece_copy(chunk, dy, x) for dy, x in partners] for chunk in range(len(CHUNKS))]
-    for group in pieces:
+    for chunk, group in enumerate(pieces):
+        if chunk:
+            arrange(chunk)
         for copy in group:
             copy.start()
     for chunk in range(len(CHUNKS)):

time: 34.2 us -> 34.1 us (level)
  no operation moved by 1% of the time
where the time goes in v4:
time: 34.1 us; the launch traced here: 34 us
  Pallas kernels  33.3 us (98%)
  between operations  0.64 us (2%)
    pallas_call x1, Pallas kernels, local(): pl.pallas_call(kernel, out_shape=(pltpu.VMEM((ROWS, TB * BLK), bf16), plt...  32.4 us
    pallas_call x1, Pallas kernels, local(): pl.pallas_call(write, out_shape=(pltpu.HBM((ROWS, TB * BLK), bf16), pltpu...  0.96 us

profile of v4, /device:TPU:1, one launch (start us, length us, event | category | flops | bytes accessed | tf_op | source)
XLA Modules:
  0.0 34.0 jit_solution(7276598548871534646)
XLA Ops:
  0.6 32.4 %coupler.1 = (bf16[192,2048]{1,0:T(8,128)(2,1)S(1)}, bf16[16,48,128]{2,1,0:T(8,128)(2,1)S(1)}) custom-call(bf16[192,512]{1,0:T(8,128)(2,1)} %phys.1, s32[1,512]{1,0:T(1,128)} %order.1, s32[16]{0:T(128)} %near_src.1, s32[4,16]{1,0:T(4,128)} %bitcast.2, bf16[16,128,128]{2,1,0:T(8,128)(2,1)} %near_w.1, bf16[16,4,128,128]{3,2,1,0:T(8,128)(2,1)} %bil_w.1, ...), custom_call_target="tpu_custom_call" | custom-call | tf_op jit(solution)/shard_map/coupler/pallas_call | solution.py:262
  33.0 1.0 %write.1 = (bf16[192,2048]{1,0:T(8,128)(2,1)}, bf16[16,48,128]{2,1,0:T(8,128)(2,1)}) custom-call(bf16[192,2048]{1,0:T(8,128)(2,1)S(1)} %get-tuple-element.4.remapped, bf16[16,48,128]{2,1,0:T(8,128)(2,1)S(1)} %get-tuple-element.5.ocean), custom_call_target="tpu_custom_call" | custom-call | tf_op jit(solution)/shard_map/write/pallas_call | solution.py:301
